TPU v7x, 512 devices: a whole 4x4x16 slice. The times are simulated.
512 devices in a mesh: mesh: 64 (over y, z), obs: 8 (over x, core).
Axes of the slice: x: 4, y: 4, z: 16, core: 2. Of those that a mesh axis runs over, the one named last changes fastest.
Arguments:
- probes: bfloat16 [64, 512, 2048], P(None, 'mesh', 'obs'), may hold values from -6 to 6
- velocity: float32 [512, 2048], P('mesh', 'obs'), may hold values from 0.5 to 2
- viscosity: float32 [512, 2048], P('mesh', 'obs'), may hold values from 0.1 to 3
- friction: float32 [512, 2048], P('mesh', 'obs'), may hold values from 0.5 to 4
- obs_block: int32 [64, 512], P('mesh', 'obs'), may hold values from 0 to 127
- obs_weight: float32 [64, 512, 128], P('mesh', 'obs'), may hold values from -0.5 to 0.5
- obs_prec: float32 [64, 512], P('mesh', 'obs'), may hold values from 0.05 to 0.5
- rank: int32 [1], replicated, may hold values from 1 to 64
Outputs:
- basis: float32 [64, 512, 2048], P(None, 'mesh', 'obs')
- factor: float32 [64, 64], replicated
All inputs are finite; a program needn't handle non-finite values.
Results may differ from a plain program's by a relative error of at most 0.0027.
Values may be sent and summed in bfloat16 or wider, within the bound.
A program may use at most 64 MiB of HBM per device.

v0:
```python
import jax
import jax.numpy as jnp
from jax import lax
from jax.sharding import PartitionSpec as P

BLOCK = 128
PRIOR = 1.0


def extended(block, sides, width):
    for axis, dim in sides:
        count = lax.axis_size(axis)
        forward = [(i, i + 1) for i in range(count - 1)]
        backward = [(target, source) for source, target in forward]
        low = lax.ppermute(
            lax.slice_in_dim(block, block.shape[dim] - width, None, axis=dim), axis, forward
        )
        high = lax.ppermute(lax.slice_in_dim(block, 0, width, axis=dim), axis, backward)
        block = jnp.concatenate([low, block, high], axis=dim)
    return block


def apply_padded(padded, visc_pad, friction):
    height = padded.shape[1] - 2
    width = padded.shape[2] - 2
    centre = padded[:, 1:-1, 1:-1]
    visc_mid = visc_pad[1:-1, 1:-1]
    result = friction * centre
    for shift_row, shift_col in ((2, 1), (0, 1), (1, 2), (1, 0)):
        neighbor = padded[:, shift_row : shift_row + height, shift_col : shift_col + width]
        face_coef = 0.5 * (
            visc_mid + visc_pad[shift_row : shift_row + height, shift_col : shift_col + width]
        )
        result = result + face_coef * (centre - neighbor)
    return result


def per_device(probes, velocity, viscosity, friction, obs_block, obs_weight, obs_prec, rank):
    probe_count = probes.shape[0]
    rows_here, cols_here = velocity.shape
    obs_devices = lax.axis_size("obs")
    slab_columns = cols_here * obs_devices // BLOCK
    owned_blocks = cols_here // BLOCK
    cell_total = rows_here * cols_here * lax.axis_size("mesh") * obs_devices
    omega = probes.astype(jnp.float32)
    stacked = jnp.concatenate([velocity[None] * omega, viscosity[None]], axis=0)
    padded = extended(stacked, (("mesh", 1), ("obs", 2)), 1)
    visc_pad = padded[-1]
    tangent = apply_padded(padded[:-1], visc_pad, friction).astype(jnp.bfloat16)
    row_ids = obs_block[0] // slab_columns
    col_ids = obs_block[0] % slab_columns
    weights = obs_weight[0]
    precision = obs_prec[0]
    segment = lax.all_gather(tangent, "obs", axis=2, tiled=True)
    seg_blocks = segment.shape[2] // BLOCK
    local_col = col_ids
    inside = (local_col >= 0) & (local_col < seg_blocks)
    block_index = row_ids * seg_blocks + jnp.clip(local_col, 0, seg_blocks - 1)
    blocks = segment.reshape(probe_count, rows_here * seg_blocks, BLOCK)
    picked = jnp.take(blocks, block_index, axis=1).astype(jnp.float32)
    value = precision * jnp.sum(picked * weights, axis=-1)
    misfit = jnp.where(inside, value, 0.0)
    amount = lax.axis_size("obs") * owned_blocks
    local_col = col_ids
    inside = (local_col >= 0) & (local_col < amount)
    block_index = jnp.clip(local_col, 0, amount - 1) * rows_here + row_ids
    contrib = jnp.where(inside[None, :, None], misfit[:, :, None] * weights[None], 0.0)
    partial_value = (
        jnp.zeros((probe_count, amount * rows_here, BLOCK), jnp.float32)
        .at[:, block_index]
        .add(contrib)
    )
    received = lax.psum_scatter(
        partial_value.reshape(probe_count, amount, rows_here, BLOCK).transpose(1, 0, 2, 3),
        "obs",
        scatter_dimension=0,
        tiled=True,
    )
    source = received.transpose(1, 2, 0, 3).reshape(probe_count, rows_here, cols_here)
    padded_source = extended(source, (("mesh", 1), ("obs", 2)), 1)
    gradient = velocity * apply_padded(padded_source, visc_pad, friction)
    sketch = (gradient + PRIOR * omega).reshape(probe_count, rows_here * cols_here)
    local_gram = (
        jnp.dot(
            sketch, sketch.T, precision=lax.Precision.HIGHEST, preferred_element_type=jnp.float32
        )
        / cell_total
    )
    factor = jnp.linalg.cholesky(lax.psum(local_gram, ("mesh", "obs")))
    solved = lax.linalg.triangular_solve(factor, sketch, left_side=True, lower=True)
    retained = (jnp.arange(probe_count, dtype=jnp.int32) < rank[0])[:, None]
    basis = jnp.where(retained, solved, 0.0).reshape(probe_count, rows_here, cols_here)
    return (basis, factor)


def solution(mesh):
    in_specs = (
        P(None, "mesh", "obs"),
        P("mesh", "obs"),
        P("mesh", "obs"),
        P("mesh", "obs"),
        P("mesh", "obs"),
        P("mesh", "obs", None),
        P("mesh", "obs"),
        P(),
    )
    out_specs = (P(None, "mesh", "obs"), P())
    return jax.shard_map(
        per_device, mesh=mesh, in_specs=in_specs, out_specs=out_specs, check_vma=False
    )
```

profile of v0, /device:TPU:1, one launch (start us, length us, event | category | flops | bytes accessed | tf_op | source)
XLA Modules:
  0.0 289.0 jit_solution(15032128486639405339)
XLA Ops:
  7.2 1.0 convert_multiply_fusion
  8.2 0.9 pad_maximum_fusion.23
  9.1 4.4 %collective-permute-start = (f32[65,1,256]{2,0,1:T(8,128)S(1)}, f32[65,1,256]{2,0,1:T(8,128)S(1)}, u32[]{:S(2)}, u32[]{:S(2)}) collective-permute-start(f32[65,1,256]{2,0,1:T(8,128)S(1)} %copy.38), channel_id=1, source_target_pairs={{0,8},{8,16},{16,24},{24,32},{32,40},{40,48},{48,56},{56,64},{64,7... | collective-permute-start | bytes 199688 | tf_op jit(solution)/shard_map/ppermute | solution.py:15
  13.5 1.3 collective-permute-start.1
  14.9 3.8 %collective-permute-done.1 = f32[65,1,256]{2,0,1:T(8,128)S(1)} collective-permute-done((f32[65,1,256]{2,0,1:T(8,128)S(1)}, f32[65,1,256]{2,0,1:T(8,128)S(1)}, u32[]{:S(2)}, u32[]{:S(2)}) %collective-permute-start.1) | collective-permute-done | bytes 66592 | tf_op jit(solution)/shard_map/ppermute | solution.py:18
  18.8 0.9 pad_maximum_fusion
  19.7 0.2 fusion.39
  20.0 0.3 copy.42
  20.2 4.9 %collective-permute-start.2 = (f32[65,10,1]{0,1,2:T(8,128)S(1)}, f32[65,10,1]{0,1,2:T(8,128)S(1)}, u32[]{:S(2)}, u32[]{:S(2)}) collective-permute-start(f32[65,10,1]{0,1,2:T(8,128)S(1)} %copy.42), channel_id=1, source_target_pairs={{0,1},{1,2},{2,3},{3,4},{4,5},{5,6},{6,7},{8,9},{9,10},{10,11},{11... | collective-permute-start | bytes 7808 | tf_op jit(solution)/shard_map/ppermute | solution.py:15
  25.2 0.3 copy.43
  25.4 3.0 %collective-permute-start.3 = (f32[65,10,1]{0,1,2:T(8,128)S(1)}, f32[65,10,1]{0,1,2:T(8,128)S(1)}, u32[]{:S(2)}, u32[]{:S(2)}) collective-permute-start(f32[65,10,1]{0,1,2:T(8,128)S(1)} %copy.43), channel_id=1, source_target_pairs={{1,0},{2,1},{3,2},{4,3},{5,4},{6,5},{7,6},{9,8},{10,9},{11,10},{12... | collective-permute-start | bytes 7808 | tf_op jit(solution)/shard_map/ppermute | solution.py:18
  28.5 0.3 copy.44
  28.8 1.6 collective-permute-done.3
  30.4 0.3 copy.45
  30.8 0.1 fusion.30
  30.9 0.1 fusion.34
  30.9 1.8 fusion.17
  32.9 38.9 %all-gather.2.cloned.1.call-done = bf16[64,8,2048]{2,1,0:T(8,128)(2,1)} async-done(((bf16[64,8,256]{2,1,0:T(8,128)(2,1)}), bf16[64,8,2048]{2,1,0:T(8,128)(2,1)}) %all-gather.2.cloned.1.call-update) | async-done | bytes 2097168 | tf_op jit(solution)/shard_map/all_gather | solution.py:54
  71.7 2.9 reshape.238
  74.6 2.7 copy.50
  77.3 2.3 gather_fusion
  79.6 0.9 multiply_reduce_fusion
  80.5 0.1 select_bitcast_fusion.1
  80.6 0.8 select_bitcast_fusion
  81.4 2.5 broadcast_in_dim.67
  83.9 9.0 %scatter_fusion = f32[64,128,128]{2,0,1:T(8,128)} fusion(f32[64,128,128]{2,0,1:T(8,128)} %broadcast_in_dim.67, s32[64]{0:T(128)S(1)} %fusion.36, f32[64,64,128]{2,1,0:T(8,128)S(1)} %select_bitcast_fusion), kind=kCustom, calls=%fused_computation.1 | custom fusion | flops 524288 | bytes 6291712 | tf_op jit(solution)/shard_map/scatter-add | solution.py:71
  92.9 44.1 %reduce-scatter.2.cloned.1.call-done = f32[2,64,8,128]{3,1,2,0:T(8,128)} async-done(((f32[16,64,8,128]{3,1,2,0:T(8,128)}), f32[2,64,8,128]{3,1,2,0:T(8,128)}) %reduce-scatter.2.cloned.1.call-update) | async-done | bytes 524304 | tf_op jit(solution)/shard_map/reduce_scatter | solution.py:73
  137.0 1.3 copy.63
  138.4 0.1 fusion.41
  138.5 1.3 collective-permute-start.4
  139.8 4.0 %collective-permute-start.5 = (f32[64,1,256]{2,1,0:T(1,128)S(1)}, f32[64,1,256]{2,1,0:T(1,128)S(1)}, u32[]{:S(2)}, u32[]{:S(2)}) collective-permute-start(f32[64,1,256]{2,1,0:T(1,128)S(1)} %get-tuple-element.13), channel_id=1, source_target_pairs={{0,8},{8,16},{16,24},{24,32},{32,40},{40,48},{48,56},{56,64},{64,7... | collective-permute-start | bytes 196616 | tf_op jit(solution)/shard_map/ppermute | solution.py:15
  144.4 0.7 collective-permute-done.5
  145.1 0.2 pad_maximum_fusion.1
  145.3 0.2 fusion.40
  145.5 6.2 %collective-permute-start.6 = (f32[64,10,1]{2,1,0:T(8,128)S(1)}, f32[64,10,1]{2,1,0:T(8,128)S(1)}, u32[]{:S(2)}, u32[]{:S(2)}) collective-permute-start(f32[64,10,1]{2,1,0:T(8,128)S(1)} %get-tuple-element.9), channel_id=1, source_target_pairs={{1,0},{2,1},{3,2},{4,3},{5,4},{6,5},{7,6},{9,8},{10,9},{11,10},{12... | collective-permute-start | bytes 7688 | tf_op jit(solution)/shard_map/ppermute | solution.py:18
  151.6 1.9 collective-permute-start.7
  153.6 2.5 collective-permute-done.6
  156.1 3.6 %collective-permute-done.7 = f32[64,10,1]{2,1,0:T(8,128)S(1)} collective-permute-done((f32[64,10,1]{2,1,0:T(8,128)S(1)}, f32[64,10,1]{2,1,0:T(8,128)S(1)}, u32[]{:S(2)}, u32[]{:S(2)}) %collective-permute-start.7) | collective-permute-done | bytes 2592 | tf_op jit(solution)/shard_map/ppermute | solution.py:15
  159.7 0.8 convert_add_fusion
  160.5 0.7 fusion
  161.2 106.3 %psum.7 = f32[64,64]{0,1:T(8,128)S(1)} all-reduce(f32[64,64]{0,1:T(8,128)S(1)} %fusion), channel_id=1, replica_groups=mesh['mesh'=64,'obs'=8] {'mesh','obs'}, use_global_device_ids=true, to_apply=%region_3.4 | all-reduce | flops 4096 | bytes 32768 | tf_op jit(solution)/shard_map/psum | solution.py:89
  267.7 5.8 %cholesky.15 = f32[64,64]{1,0:T(8,128)S(1)} custom-call(f32[64,64]{1,0:T(8,128)S(1)} %fusion.29), custom_call_target="Cholesky" | custom-call | tf_op jit(solution)/shard_map/jit(cholesky)/cholesky | solution.py:89
  273.5 0.6 compare_reduce_fusion
  274.2 1.3 select_bitcast_fusion.2
  275.4 4.9 %custom-call.6 = f32[1,64,64]{1,2,0:T(8,128)S(1)} custom-call(f32[1,64,64]{2,1,0:T(8,128)S(1)} %get-tuple-element.2), custom_call_target="InvertDiagBlocksLowerTriangular" | custom-call | tf_op jit(solution)/shard_map/triangular_solve | solution.py:90
  280.3 0.2 copy.58
  280.5 0.6 convolution_select_fusion
  281.2 1.0 copy.59
  (33 shorter events, 0.5 us)
Async XLA Ops:
  7.2 64.5 %all-gather.2.cloned.1.call-start = ((), (), s32[]{:S(2)}) async-start(), calls=%async_computation.1 | async-start | bytes 2359296 | tf_op jit(solution)/shard_map/all_gather | solution.py:54
  9.1 5.8 %collective-permute-start = (f32[65,1,256]{2,0,1:T(8,128)S(1)}, f32[65,1,256]{2,0,1:T(8,128)S(1)}, u32[]{:S(2)}, u32[]{:S(2)}) collective-permute-start(f32[65,1,256]{2,0,1:T(8,128)S(1)} %copy.38), channel_id=1, source_target_pairs={{0,8},{8,16},{16,24},{24,32},{32,40},{40,48},{48,56},{56,64},{64,7... | collective-permute-start | bytes 199688 | tf_op jit(solution)/shard_map/ppermute | solution.py:15
  13.5 5.3 %collective-permute-start.1 = (f32[65,1,256]{2,0,1:T(8,128)S(1)}, f32[65,1,256]{2,0,1:T(8,128)S(1)}, u32[]{:S(2)}, u32[]{:S(2)}) collective-permute-start(f32[65,1,256]{2,0,1:T(8,128)S(1)} %copy.39), channel_id=1, source_target_pairs={{8,0},{16,8},{24,16},{32,24},{40,32},{48,40},{56,48},{64,56},{72,6... | collective-permute-start | bytes 199688 | tf_op jit(solution)/shard_map/ppermute | solution.py:18
  19.7 11.0 %copy-start.2 = (f32[8,256]{1,0:T(8,128)S(1)}, f32[8,256]{1,0:T(8,128)}, u32[]{:S(2)}) copy-start(f32[8,256]{1,0:T(8,128)} %param.10) | copy-start | bytes 24580
  19.9 11.0 %copy-start.4 = (f32[8,256]{1,0:T(8,128)S(1)}, f32[8,256]{1,0:T(8,128)}, u32[]{:S(2)}) copy-start(f32[8,256]{1,0:T(8,128)} %param.11) | copy-start | bytes 24580
  20.2 8.2 %collective-permute-start.2 = (f32[65,10,1]{0,1,2:T(8,128)S(1)}, f32[65,10,1]{0,1,2:T(8,128)S(1)}, u32[]{:S(2)}, u32[]{:S(2)}) collective-permute-start(f32[65,10,1]{0,1,2:T(8,128)S(1)} %copy.42), channel_id=1, source_target_pairs={{0,1},{1,2},{2,3},{3,4},{4,5},{5,6},{6,7},{8,9},{9,10},{10,11},{11... | collective-permute-start | bytes 7808 | tf_op jit(solution)/shard_map/ppermute | solution.py:15
  25.4 5.0 %collective-permute-start.3 = (f32[65,10,1]{0,1,2:T(8,128)S(1)}, f32[65,10,1]{0,1,2:T(8,128)S(1)}, u32[]{:S(2)}, u32[]{:S(2)}) collective-permute-start(f32[65,10,1]{0,1,2:T(8,128)S(1)} %copy.43), channel_id=1, source_target_pairs={{1,0},{2,1},{3,2},{4,3},{5,4},{6,5},{7,6},{9,8},{10,9},{11,10},{12... | collective-permute-start | bytes 7808 | tf_op jit(solution)/shard_map/ppermute | solution.py:18
  30.8 2.0 copy-start.6
  32.7 104.3 %reduce-scatter.2.cloned.1.call-start = ((), (), s32[]{:S(2)}) async-start(), calls=%async_computation.2 | async-start | bytes 4718592 | tf_op jit(solution)/shard_map/reduce_scatter | solution.py:73
  77.3 2.4 copy-start.1
  77.3 3.2 %copy-start.5 = (f32[1,64]{1,0:T(1,128)S(1)}, f32[1,64]{1,0:T(1,128)}, u32[]{:S(2)}) copy-start(f32[1,64]{1,0:T(1,128)} %param.14) | copy-start | bytes 772
  138.3 21.3 %copy-start = (bf16[64,8,256]{2,1,0:T(8,128)(2,1)S(1)}, bf16[64,8,256]{2,1,0:T(8,128)(2,1)}, u32[]{:S(2)}) copy-start(bf16[64,8,256]{2,1,0:T(8,128)(2,1)} %param.8) | copy-start | bytes 786436
  138.4 21.3 %copy-start.3 = (f32[8,256]{1,0:T(8,128)S(1)}, f32[8,256]{1,0:T(8,128)}, u32[]{:S(2)}) copy-start(f32[8,256]{1,0:T(8,128)} %param.9) | copy-start | bytes 24580
  138.5 5.9 %collective-permute-start.4 = (f32[64,1,256]{2,1,0:T(1,128)S(1)}, f32[64,1,256]{2,1,0:T(1,128)S(1)}, u32[]{:S(2)}, u32[]{:S(2)}) collective-permute-start(f32[64,1,256]{2,1,0:T(1,128)S(1)} %get-tuple-element.14), channel_id=1, source_target_pairs={{8,0},{16,8},{24,16},{32,24},{40,32},{48,40},{56,48},{64,56},{72,6... | collective-permute-start | bytes 196616 | tf_op jit(solution)/shard_map/ppermute | solution.py:18
  139.8 5.3 %collective-permute-start.5 = (f32[64,1,256]{2,1,0:T(1,128)S(1)}, f32[64,1,256]{2,1,0:T(1,128)S(1)}, u32[]{:S(2)}, u32[]{:S(2)}) collective-permute-start(f32[64,1,256]{2,1,0:T(1,128)S(1)} %get-tuple-element.13), channel_id=1, source_target_pairs={{0,8},{8,16},{16,24},{24,32},{32,40},{40,48},{48,56},{56,64},{64,7... | collective-permute-start | bytes 196616 | tf_op jit(solution)/shard_map/ppermute | solution.py:15
  145.5 10.6 %collective-permute-start.6 = (f32[64,10,1]{2,1,0:T(8,128)S(1)}, f32[64,10,1]{2,1,0:T(8,128)S(1)}, u32[]{:S(2)}, u32[]{:S(2)}) collective-permute-start(f32[64,10,1]{2,1,0:T(8,128)S(1)} %get-tuple-element.9), channel_id=1, source_target_pairs={{1,0},{2,1},{3,2},{4,3},{5,4},{6,5},{7,6},{9,8},{10,9},{11,10},{12... | collective-permute-start | bytes 7688 | tf_op jit(solution)/shard_map/ppermute | solution.py:18
  151.6 8.0 %collective-permute-start.7 = (f32[64,10,1]{2,1,0:T(8,128)S(1)}, f32[64,10,1]{2,1,0:T(8,128)S(1)}, u32[]{:S(2)}, u32[]{:S(2)}) collective-permute-start(f32[64,10,1]{2,1,0:T(8,128)S(1)} %get-tuple-element.10), channel_id=1, source_target_pairs={{0,1},{1,2},{2,3},{3,4},{4,5},{5,6},{6,7},{8,9},{9,10},{10,11},{11... | collective-permute-start | bytes 7688 | tf_op jit(solution)/shard_map/ppermute | solution.py:15
Sparse Core Ops, SparseCore 0:
  32.8 38.8 all-gather.1
  93.0 43.9 reduce-scatter.1
where the time goes:
time: 290 us; the launch traced here: 289 us
  blocking collectives  106 us (37%)
  waiting for transfers between devices  95.2 us (33%)
  other arithmetic  29.1 us (10%)
  starting transfers between devices  27 us (9%)
  between operations  15 us (5%)
  local copies, waits for them, and re-layouts  14.9 us (5%)
    psum x1, blocking collectives, per_device(): factor = jnp.linalg.cholesky(lax.psum(local_gram, ('mesh', 'obs')))  106 us
    reduce_scatter x1, waiting for transfers between devices, per_device(): lax.psum_scatter(partial_value.reshape(probe_count, amount, rows_here, BL...  44.1 us
    all_gather x1, waiting for transfers between devices, per_device(): segment = lax.all_gather(tangent, 'obs', axis=2, tiled=True)  38.9 us
    ppermute x4, starting transfers between devices, extended(): lax.ppermute(lax.slice_in_dim(block, block.shape[dim] - width, None, axis...  15.2 us
    ppermute x4, starting transfers between devices, extended(): lax.ppermute(lax.slice_in_dim(block, 0, width, axis=dim), axis, backward)  11.8 us
    scatter-add x1, other arithmetic, per_device(): partial_value = jnp.zeros((probe_count, amount * rows_here, BLOCK), jnp.f...  9.02 us
    ppermute x4, waiting for transfers between devices, extended(): lax.ppermute(lax.slice_in_dim(block, 0, width, axis=dim), axis, backward)  7.92 us
    another operation x3, other arithmetic, per_device(): factor = jnp.linalg.cholesky(lax.psum(local_gram, ('mesh', 'obs')))  6.52 us
  transfers between devices with their start and end apart: 10, of which 8 were waited for; matrix products, arithmetic and copies ran while one was open for 0% of the time, Pallas kernels for 0%

commit v1 on v0

--- a/solution.py
+++ b/solution.py
@@ -51,7 +51,36 @@
     col_ids = obs_block[0] % slab_columns
     weights = obs_weight[0]
     precision = obs_prec[0]
-    segment = lax.all_gather(tangent, "obs", axis=2, tiled=True)
+    response = lax.psum(1, "obs")
+    all_rows, all_values, right_arr = (response, lax.axis_index("obs"), tangent.shape[2])
+    history = []
+    for src_i, j0 in enumerate(tangent.shape):
+        history.append(j0 * all_rows if src_i == 2 else j0)
+    fresh = jnp.zeros(history, tangent.dtype)
+    segment = lax.dynamic_update_slice_in_dim(fresh, tangent, all_values * right_arr, axis=2)
+    p = 1
+    extra = view_out = tangent
+    while p < all_rows // 2 + 1:
+        ledger = []
+        src_i = 0
+        while src_i < all_rows:
+            ledger.append((src_i, (src_i + 1) % all_rows))
+            src_i = src_i + 1
+        extra = lax.ppermute(extra, "obs", ledger)
+        segment = lax.dynamic_update_slice_in_dim(
+            segment, extra, (all_values - p) % all_rows * right_arr, axis=2
+        )
+        if 2 * p < all_rows:
+            made = []
+            src_i = 0
+            while src_i < all_rows:
+                made.append((src_i, (src_i - 1) % all_rows))
+                src_i += 1
+            view_out = lax.ppermute(view_out, "obs", made)
+            segment = lax.dynamic_update_slice_in_dim(
+                segment, view_out, (all_values + p) % all_rows * right_arr, axis=2
+            )
+        p += 1
     seg_blocks = segment.shape[2] // BLOCK
     local_col = col_ids
     inside = (local_col >= 0) & (local_col < seg_blocks)

time: 290 us -> 277 us (0.955)
  waiting for transfers between devices: 95.2 us -> 73.1 us
  starting transfers between devices: 27 us -> 36.7 us
    all_gather x1 -> x0, waiting for transfers between devices: 38.9 us -> none  [per_device(): segment = lax.all_gather(tangent, 'obs', axis=2, tiled=True)]
    ppermute x0 -> x7, waiting for transfers between devices: none -> 11.3 us  [the longest x4 10.5 us: per_device(): extra = lax.ppermute(extra, 'obs', ledger)]
    ppermute x0 -> x7, starting transfers between devices: none -> 9.73 us  [the longest x4 7.49 us: per_device(): extra = lax.ppermute(extra, 'obs', ledger)]
    reduce_scatter x1, waiting for transfers between devices: 44.1 us -> 49.6 us  [per_device(): lax.psum_scatter(partial_value.reshape(probe_count, amount, rows_here, BL...]
  transfers between devices with their start and end apart: 10 -> 16, of which waited for: 8 -> 13; matrix products, arithmetic and copies ran while one was open for 0% -> 0% of each run, Pallas kernels for 0% -> 0%
where the time goes in v1:
time: 277 us; the launch traced here: 276 us
  blocking collectives  106 us (38%)
  waiting for transfers between devices  73.1 us (26%)
  starting transfers between devices  36.7 us (13%)
  other arithmetic  28.5 us (10%)
  between operations  15.1 us (5%)
  local copies, waits for them, and re-layouts  14.9 us (5%)
    psum x1, blocking collectives, per_device(): factor = jnp.linalg.cholesky(lax.psum(local_gram, ('mesh', 'obs')))  106 us
    reduce_scatter x1, waiting for transfers between devices, per_device(): lax.psum_scatter(partial_value.reshape(probe_count, amount, rows_here, BL...  49.6 us
    ppermute x4, starting transfers between devices, extended(): lax.ppermute(lax.slice_in_dim(block, block.shape[dim] - width, None, axis...  15.2 us
    ppermute x4, starting transfers between devices, extended(): lax.ppermute(lax.slice_in_dim(block, 0, width, axis=dim), axis, backward)  11.7 us
    ppermute x4, waiting for transfers between devices, per_device(): extra = lax.ppermute(extra, 'obs', ledger)  10.5 us
    scatter-add x1, other arithmetic, per_device(): partial_value = jnp.zeros((probe_count, amount * rows_here, BLOCK), jnp.f...  9.07 us
    ppermute x4, waiting for transfers between devices, extended(): lax.ppermute(lax.slice_in_dim(block, 0, width, axis=dim), axis, backward)  7.94 us
    ppermute x4, starting transfers between devices, per_device(): extra = lax.ppermute(extra, 'obs', ledger)  7.49 us
  transfers between devices with their start and end apart: 16, of which 13 were waited for; matrix products, arithmetic and copies ran while one was open for 0% of the time, Pallas kernels for 0%

profile of v1, /device:TPU:1, one launch (start us, length us, event | category | flops | bytes accessed | tf_op | source)
XLA Modules:
  0.0 276.0 jit_solution(1124678791842772861)
XLA Ops:
  7.2 1.0 convert_multiply_fusion
  8.2 0.9 pad_maximum_fusion.23
  9.1 4.4 %collective-permute-start = (f32[65,1,256]{2,0,1:T(8,128)S(1)}, f32[65,1,256]{2,0,1:T(8,128)S(1)}, u32[]{:S(2)}, u32[]{:S(2)}) collective-permute-start(f32[65,1,256]{2,0,1:T(8,128)S(1)} %copy.45), channel_id=1, source_target_pairs={{0,8},{8,16},{16,24},{24,32},{32,40},{40,48},{48,56},{56,64},{64,7... | collective-permute-start | bytes 199688 | tf_op jit(solution)/shard_map/ppermute | solution.py:15
  13.5 1.3 collective-permute-start.1
  14.9 3.8 %collective-permute-done.1 = f32[65,1,256]{2,0,1:T(8,128)S(1)} collective-permute-done((f32[65,1,256]{2,0,1:T(8,128)S(1)}, f32[65,1,256]{2,0,1:T(8,128)S(1)}, u32[]{:S(2)}, u32[]{:S(2)}) %collective-permute-start.1) | collective-permute-done | bytes 66592 | tf_op jit(solution)/shard_map/ppermute | solution.py:18
  18.8 0.9 pad_maximum_fusion
  20.2 4.9 %collective-permute-start.2 = (f32[65,10,1]{0,1,2:T(8,128)S(1)}, f32[65,10,1]{0,1,2:T(8,128)S(1)}, u32[]{:S(2)}, u32[]{:S(2)}) collective-permute-start(f32[65,10,1]{0,1,2:T(8,128)S(1)} %copy.49), channel_id=1, source_target_pairs={{0,1},{1,2},{2,3},{3,4},{4,5},{5,6},{6,7},{8,9},{9,10},{10,11},{11... | collective-permute-start | bytes 7808 | tf_op jit(solution)/shard_map/ppermute | solution.py:15
  25.4 3.0 %collective-permute-start.3 = (f32[65,10,1]{0,1,2:T(8,128)S(1)}, f32[65,10,1]{0,1,2:T(8,128)S(1)}, u32[]{:S(2)}, u32[]{:S(2)}) collective-permute-start(f32[65,10,1]{0,1,2:T(8,128)S(1)} %copy.50), channel_id=1, source_target_pairs={{1,0},{2,1},{3,2},{4,3},{5,4},{6,5},{7,6},{9,8},{10,9},{11,10},{12... | collective-permute-start | bytes 7808 | tf_op jit(solution)/shard_map/ppermute | solution.py:18
  28.8 1.6 collective-permute-done.3
  30.9 0.6 copy-done
  31.8 0.8 copy-done.1
  32.6 1.1 constant_dynamic-update-slice_fusion.7
  33.8 0.5 collective-permute-start.5
  34.3 2.8 %collective-permute-done.4 = bf16[64,8,256]{2,1,0:T(8,128)(2,1)S(1)} collective-permute-done((bf16[64,8,256]{2,1,0:T(8,128)(2,1)S(1)}, bf16[64,8,256]{2,1,0:T(8,128)(2,1)S(1)}, u32[]{:S(2)}, u32[]{:S(2)}) %collective-permute-start.4) | collective-permute-done | bytes 262176 | tf_op jit(solution)/shard_map/ppermute | solution.py:69
  37.1 2.5 collective-permute-start.6
  39.6 0.4 collective-permute-start.7
  40.0 2.9 %collective-permute-done.6 = bf16[64,8,256]{2,1,0:T(8,128)(2,1)S(1)} collective-permute-done((bf16[64,8,256]{2,1,0:T(8,128)(2,1)S(1)}, bf16[64,8,256]{2,1,0:T(8,128)(2,1)S(1)}, u32[]{:S(2)}, u32[]{:S(2)}) %collective-permute-start.6) | collective-permute-done | bytes 262176 | tf_op jit(solution)/shard_map/ppermute | solution.py:69
  42.9 2.5 collective-permute-start.8
  45.7 1.4 collective-permute-start.9
  47.1 1.6 collective-permute-done.8
  48.7 2.5 collective-permute-start.10
  51.2 0.6 collective-permute-done.9
  51.8 3.2 %collective-permute-done.10 = bf16[64,8,256]{2,1,0:T(8,128)(2,1)S(1)} collective-permute-done((bf16[64,8,256]{2,1,0:T(8,128)(2,1)S(1)}, bf16[64,8,256]{2,1,0:T(8,128)(2,1)S(1)}, u32[]{:S(2)}, u32[]{:S(2)}) %collective-permute-start.10) | collective-permute-done | bytes 262176 | tf_op jit(solution)/shard_map/ppermute | solution.py:69
  55.0 2.4 reshape.238
  57.4 2.9 %copy.57 = bf16[64,128,128]{2,0,1:T(8,128)(2,1)S(1)} copy(bf16[64,128,128]{2,1,0:T(8,128)(2,1)} %reshape.238) | data formatting | bytes 4194304 | tf_op jit(solution)/shard_map/reshape | solution.py:88
  60.4 0.7 gather_fusion
  61.1 0.9 multiply_reduce_fusion
  62.1 0.8 select_bitcast_fusion
  62.9 2.5 broadcast_in_dim.70
  65.3 9.1 %scatter_fusion = f32[64,128,128]{2,0,1:T(8,128)} fusion(f32[64,128,128]{2,0,1:T(8,128)} %broadcast_in_dim.70, s32[64]{0:T(128)S(1)} %fusion.36, f32[64,64,128]{2,1,0:T(8,128)S(1)} %select_bitcast_fusion), kind=kCustom, calls=%fused_computation.1 | custom fusion | flops 524288 | bytes 6291712 | tf_op jit(solution)/shard_map/scatter-add | solution.py:100
  74.4 49.6 %reduce-scatter.2.cloned.1.call-done = f32[2,64,8,128]{3,1,2,0:T(8,128)} async-done(((f32[16,64,8,128]{3,1,2,0:T(8,128)}), f32[2,64,8,128]{3,1,2,0:T(8,128)}) %reduce-scatter.2.cloned.1.call-update) | async-done | bytes 524304 | tf_op jit(solution)/shard_map/reduce_scatter | solution.py:102
  124.0 1.3 copy.70
  125.5 1.3 collective-permute-start.11
  126.8 4.0 %collective-permute-start.12 = (f32[64,1,256]{2,1,0:T(1,128)S(1)}, f32[64,1,256]{2,1,0:T(1,128)S(1)}, u32[]{:S(2)}, u32[]{:S(2)}) collective-permute-start(f32[64,1,256]{2,1,0:T(1,128)S(1)} %get-tuple-element.15), channel_id=1, source_target_pairs={{0,8},{8,16},{16,24},{24,32},{32,40},{40,48},{48,56},{56,64},{64,7... | collective-permute-start | bytes 196616 | tf_op jit(solution)/shard_map/ppermute | solution.py:15
  131.4 0.7 collective-permute-done.12
  132.5 6.1 %collective-permute-start.13 = (f32[64,10,1]{2,1,0:T(8,128)S(1)}, f32[64,10,1]{2,1,0:T(8,128)S(1)}, u32[]{:S(2)}, u32[]{:S(2)}) collective-permute-start(f32[64,10,1]{2,1,0:T(8,128)S(1)} %get-tuple-element.11), channel_id=1, source_target_pairs={{1,0},{2,1},{3,2},{4,3},{5,4},{6,5},{7,6},{9,8},{10,9},{11,10},{12... | collective-permute-start | bytes 7688 | tf_op jit(solution)/shard_map/ppermute | solution.py:18
  138.6 1.9 collective-permute-start.14
  140.6 2.5 collective-permute-done.13
  143.1 3.6 %collective-permute-done.14 = f32[64,10,1]{2,1,0:T(8,128)S(1)} collective-permute-done((f32[64,10,1]{2,1,0:T(8,128)S(1)}, f32[64,10,1]{2,1,0:T(8,128)S(1)}, u32[]{:S(2)}, u32[]{:S(2)}) %collective-permute-start.14) | collective-permute-done | bytes 2592 | tf_op jit(solution)/shard_map/ppermute | solution.py:15
  146.6 0.8 convert_add_fusion
  147.5 0.7 fusion
  148.2 106.4 %psum.7 = f32[64,64]{0,1:T(8,128)S(1)} all-reduce(f32[64,64]{0,1:T(8,128)S(1)} %fusion), channel_id=1, replica_groups=mesh['mesh'=64,'obs'=8] {'mesh','obs'}, use_global_device_ids=true, to_apply=%region_3.4 | all-reduce | flops 4096 | bytes 32768 | tf_op jit(solution)/shard_map/psum | solution.py:118
  254.7 5.8 %cholesky.15 = f32[64,64]{1,0:T(8,128)S(1)} custom-call(f32[64,64]{1,0:T(8,128)S(1)} %fusion.29), custom_call_target="Cholesky" | custom-call | tf_op jit(solution)/shard_map/jit(cholesky)/cholesky | solution.py:118
  260.6 0.6 compare_reduce_fusion
  261.2 1.3 select_bitcast_fusion.2
  262.5 4.9 %custom-call.6 = f32[1,64,64]{1,2,0:T(8,128)S(1)} custom-call(f32[1,64,64]{2,1,0:T(8,128)S(1)} %get-tuple-element.2), custom_call_target="InvertDiagBlocksLowerTriangular" | custom-call | tf_op jit(solution)/shard_map/triangular_solve | solution.py:119
  267.6 0.6 convolution_select_fusion
  268.2 1.0 copy.66
  (56 shorter events, 3.6 us)
Async XLA Ops:
  7.2 116.8 %reduce-scatter.2.cloned.1.call-start = ((), (), s32[]{:S(2)}) async-start(), calls=%async_computation.1 | async-start | bytes 4718592 | tf_op jit(solution)/shard_map/reduce_scatter | solution.py:102
  9.1 5.8 %collective-permute-start = (f32[65,1,256]{2,0,1:T(8,128)S(1)}, f32[65,1,256]{2,0,1:T(8,128)S(1)}, u32[]{:S(2)}, u32[]{:S(2)}) collective-permute-start(f32[65,1,256]{2,0,1:T(8,128)S(1)} %copy.45), channel_id=1, source_target_pairs={{0,8},{8,16},{16,24},{24,32},{32,40},{40,48},{48,56},{56,64},{64,7... | collective-permute-start | bytes 199688 | tf_op jit(solution)/shard_map/ppermute | solution.py:15
  13.5 5.3 %collective-permute-start.1 = (f32[65,1,256]{2,0,1:T(8,128)S(1)}, f32[65,1,256]{2,0,1:T(8,128)S(1)}, u32[]{:S(2)}, u32[]{:S(2)}) collective-permute-start(f32[65,1,256]{2,0,1:T(8,128)S(1)} %copy.46), channel_id=1, source_target_pairs={{8,0},{16,8},{24,16},{32,24},{40,32},{48,40},{56,48},{64,56},{72,6... | collective-permute-start | bytes 199688 | tf_op jit(solution)/shard_map/ppermute | solution.py:18
  19.7 11.0 %copy-start.4 = (f32[8,256]{1,0:T(8,128)S(1)}, f32[8,256]{1,0:T(8,128)}, u32[]{:S(2)}) copy-start(f32[8,256]{1,0:T(8,128)} %param.10) | copy-start | bytes 24580
  20.2 8.2 %collective-permute-start.2 = (f32[65,10,1]{0,1,2:T(8,128)S(1)}, f32[65,10,1]{0,1,2:T(8,128)S(1)}, u32[]{:S(2)}, u32[]{:S(2)}) collective-permute-start(f32[65,10,1]{0,1,2:T(8,128)S(1)} %copy.49), channel_id=1, source_target_pairs={{0,1},{1,2},{2,3},{3,4},{4,5},{5,6},{6,7},{8,9},{9,10},{10,11},{11... | collective-permute-start | bytes 7808 | tf_op jit(solution)/shard_map/ppermute | solution.py:15
  25.4 5.0 %collective-permute-start.3 = (f32[65,10,1]{0,1,2:T(8,128)S(1)}, f32[65,10,1]{0,1,2:T(8,128)S(1)}, u32[]{:S(2)}, u32[]{:S(2)}) collective-permute-start(f32[65,10,1]{0,1,2:T(8,128)S(1)} %copy.50), channel_id=1, source_target_pairs={{1,0},{2,1},{3,2},{4,3},{5,4},{6,5},{7,6},{9,8},{10,9},{11,10},{12... | collective-permute-start | bytes 7808 | tf_op jit(solution)/shard_map/ppermute | solution.py:18
  30.8 0.8 copy-start
  30.8 1.1 copy-start.6
  31.6 1.0 copy-start.1
  31.6 2.2 copy-start.8
  33.7 3.4 %collective-permute-start.4 = (bf16[64,8,256]{2,1,0:T(8,128)(2,1)S(1)}, bf16[64,8,256]{2,1,0:T(8,128)(2,1)S(1)}, u32[]{:S(2)}, u32[]{:S(2)}) collective-permute-start(bf16[64,8,256]{2,1,0:T(8,128)(2,1)S(1)} %get-tuple-element.8), channel_id=1, source_target_pairs={{0,1},{1,2},{2,3},{3,4},{4,5},{5,6},{6,7},{7,0},{8,9},{9,10},{10,1... | collective-permute-start | bytes 786440 | tf_op jit(solution)/shard_map/ppermute | solution.py:69
  33.8 5.8 %collective-permute-start.5 = (bf16[64,8,256]{2,1,0:T(8,128)(2,1)S(1)}, bf16[64,8,256]{2,1,0:T(8,128)(2,1)S(1)}, u32[]{:S(2)}, u32[]{:S(2)}) collective-permute-start(bf16[64,8,256]{2,1,0:T(8,128)(2,1)S(1)} %get-tuple-element.8), channel_id=1, source_target_pairs={{0,7},{1,0},{2,1},{3,2},{4,3},{5,4},{6,5},{7,6},{8,15},{9,8},{10,9... | collective-permute-start | bytes 786440 | tf_op jit(solution)/shard_map/ppermute | solution.py:79
  37.1 5.8 %collective-permute-start.6 = (bf16[64,8,256]{2,1,0:T(8,128)(2,1)S(1)}, bf16[64,8,256]{2,1,0:T(8,128)(2,1)S(1)}, u32[]{:S(2)}, u32[]{:S(2)}) collective-permute-start(bf16[64,8,256]{2,1,0:T(8,128)(2,1)S(1)} %collective-permute-done.4), channel_id=1, source_target_pairs={{0,1},{1,2},{2,3},{3,4},{4,5},{5,6},{6,7},{7,0},{8,9},{9,10},{10,1... | collective-permute-start | bytes 786440 | tf_op jit(solution)/shard_map/ppermute | solution.py:69
  39.6 6.1 %collective-permute-start.7 = (bf16[64,8,256]{2,1,0:T(8,128)(2,1)S(1)}, bf16[64,8,256]{2,1,0:T(8,128)(2,1)S(1)}, u32[]{:S(2)}, u32[]{:S(2)}) collective-permute-start(bf16[64,8,256]{2,1,0:T(8,128)(2,1)S(1)} %collective-permute-done.5), channel_id=1, source_target_pairs={{0,7},{1,0},{2,1},{3,2},{4,3},{5,4},{6,5},{7,6},{8,15},{9,8},{10,9... | collective-permute-start | bytes 786440 | tf_op jit(solution)/shard_map/ppermute | solution.py:79
  42.9 5.8 %collective-permute-start.8 = (bf16[64,8,256]{2,1,0:T(8,128)(2,1)S(1)}, bf16[64,8,256]{2,1,0:T(8,128)(2,1)S(1)}, u32[]{:S(2)}, u32[]{:S(2)}) collective-permute-start(bf16[64,8,256]{2,1,0:T(8,128)(2,1)S(1)} %collective-permute-done.6), channel_id=1, source_target_pairs={{0,1},{1,2},{2,3},{3,4},{4,5},{5,6},{6,7},{7,0},{8,9},{9,10},{10,1... | collective-permute-start | bytes 786440 | tf_op jit(solution)/shard_map/ppermute | solution.py:69
  45.7 6.1 %collective-permute-start.9 = (bf16[64,8,256]{2,1,0:T(8,128)(2,1)S(1)}, bf16[64,8,256]{2,1,0:T(8,128)(2,1)S(1)}, u32[]{:S(2)}, u32[]{:S(2)}) collective-permute-start(bf16[64,8,256]{2,1,0:T(8,128)(2,1)S(1)} %collective-permute-done.7), channel_id=1, source_target_pairs={{0,7},{1,0},{2,1},{3,2},{4,3},{5,4},{6,5},{7,6},{8,15},{9,8},{10,9... | collective-permute-start | bytes 786440 | tf_op jit(solution)/shard_map/ppermute | solution.py:79
  48.7 6.3 %collective-permute-start.10 = (bf16[64,8,256]{2,1,0:T(8,128)(2,1)S(1)}, bf16[64,8,256]{2,1,0:T(8,128)(2,1)S(1)}, u32[]{:S(2)}, u32[]{:S(2)}) collective-permute-start(bf16[64,8,256]{2,1,0:T(8,128)(2,1)S(1)} %collective-permute-done.8), channel_id=1, source_target_pairs={{0,1},{1,2},{2,3},{3,4},{4,5},{5,6},{6,7},{7,0},{8,9},{9,10},{10,1... | collective-permute-start | bytes 786440 | tf_op jit(solution)/shard_map/ppermute | solution.py:69
  60.3 0.8 copy-start.3
  60.3 1.7 copy-start.7
  125.3 21.3 %copy-start.2 = (bf16[64,8,256]{2,1,0:T(8,128)(2,1)S(1)}, bf16[64,8,256]{2,1,0:T(8,128)(2,1)}, u32[]{:S(2)}) copy-start(bf16[64,8,256]{2,1,0:T(8,128)(2,1)} %param.8) | copy-start | bytes 786436
  125.4 21.3 %copy-start.5 = (f32[8,256]{1,0:T(8,128)S(1)}, f32[8,256]{1,0:T(8,128)}, u32[]{:S(2)}) copy-start(f32[8,256]{1,0:T(8,128)} %param.9) | copy-start | bytes 24580
  125.5 5.9 %collective-permute-start.11 = (f32[64,1,256]{2,1,0:T(1,128)S(1)}, f32[64,1,256]{2,1,0:T(1,128)S(1)}, u32[]{:S(2)}, u32[]{:S(2)}) collective-permute-start(f32[64,1,256]{2,1,0:T(1,128)S(1)} %get-tuple-element.16), channel_id=1, source_target_pairs={{8,0},{16,8},{24,16},{32,24},{40,32},{48,40},{56,48},{64,56},{72,6... | collective-permute-start | bytes 196616 | tf_op jit(solution)/shard_map/ppermute | solution.py:18
  126.8 5.3 %collective-permute-start.12 = (f32[64,1,256]{2,1,0:T(1,128)S(1)}, f32[64,1,256]{2,1,0:T(1,128)S(1)}, u32[]{:S(2)}, u32[]{:S(2)}) collective-permute-start(f32[64,1,256]{2,1,0:T(1,128)S(1)} %get-tuple-element.15), channel_id=1, source_target_pairs={{0,8},{8,16},{16,24},{24,32},{32,40},{40,48},{48,56},{56,64},{64,7... | collective-permute-start | bytes 196616 | tf_op jit(solution)/shard_map/ppermute | solution.py:15
  132.5 10.6 %collective-permute-start.13 = (f32[64,10,1]{2,1,0:T(8,128)S(1)}, f32[64,10,1]{2,1,0:T(8,128)S(1)}, u32[]{:S(2)}, u32[]{:S(2)}) collective-permute-start(f32[64,10,1]{2,1,0:T(8,128)S(1)} %get-tuple-element.11), channel_id=1, source_target_pairs={{1,0},{2,1},{3,2},{4,3},{5,4},{6,5},{7,6},{9,8},{10,9},{11,10},{12... | collective-permute-start | bytes 7688 | tf_op jit(solution)/shard_map/ppermute | solution.py:18
  138.6 8.0 %collective-permute-start.14 = (f32[64,10,1]{2,1,0:T(8,128)S(1)}, f32[64,10,1]{2,1,0:T(8,128)S(1)}, u32[]{:S(2)}, u32[]{:S(2)}) collective-permute-start(f32[64,10,1]{2,1,0:T(8,128)S(1)} %get-tuple-element.12), channel_id=1, source_target_pairs={{0,1},{1,2},{2,3},{3,4},{4,5},{5,6},{6,7},{8,9},{9,10},{10,11},{11... | collective-permute-start | bytes 7688 | tf_op jit(solution)/shard_map/ppermute | solution.py:15
Sparse Core Ops, SparseCore 0:
  74.6 49.3 reduce-scatter.1
